TPU v7x, 32 devices: a whole 2x2x4 slice. The times are simulated.
32 devices in a mesh: row: 8 (over z, y), col: 4 (over x, core).
Axes of the slice: x: 2, y: 2, z: 4, core: 2. Of those that a mesh axis runs over, the one named last changes fastest.
Arguments:
- trailing: float32 [16384, 16384], P('row', 'col'), may hold values from -40 to 40, as said below
- factor_one: float32 [16384, 512], P(('row', 'col')), may hold values from -0.0390625 to 0.0390625
- inverse_one: float32 [512, 512], replicated, may hold values from -1 to 2, as said below
- factor_two_top: float32 [512, 512], replicated, may hold values from -0.0390625 to 0.0390625
- factor_two: float32 [16384, 512], P(('row', 'col')), may hold values from -0.0390625 to 0.0390625
- inverse_two: float32 [512, 512], replicated, may hold values from -1 to 2, as said below
- structure_one: int32 [96], replicated, may hold values from 0 to 127, as said below
- structure_two: int32 [94], replicated, may hold values from 0 to 127, as said below
Outputs:
- column_one: float32 [16384, 512], P(('row', 'col'))
- diagonal_one: float32 [512, 512], replicated
- column_two: float32 [16384, 512], P(('row', 'col'))
- cross_two: float32 [512, 512], replicated
- diagonal_two: float32 [512, 512], replicated
Inputs may be any that keep to these rules, and one draw needn't show every extreme that they name: `trailing`: symmetric. `inverse_one`: lower triangular, diagonal between 1 and 2. `inverse_two`: lower triangular, diagonal between 1 and 2. `structure_one`: distinct, rising; lists block 0 and the last block. `structure_two`: distinct, rising, each also listed in structure_one; lists block 0 and the last block.
All inputs are finite; a program needn't handle non-finite values.
Results may differ from a plain program's by a relative error of at most 0.0003.
Values sent between devices are 32-bit elements; how exact they have to be, the bound alone decides.
A program may use at most 128 MiB of HBM per device.

v0:
```python
import jax
import jax.numpy as jnp
from jax import lax
from jax.sharding import PartitionSpec as P

BLK = 128


def spread(x, axis, root):
    mine = lax.axis_index(axis) == root
    return lax.psum(jnp.where(mine, x, jnp.zeros_like(x)), axis)


def product(left, right):
    return jnp.dot(left, right, precision=lax.Precision.HIGHEST, preferred_element_type=jnp.float32)


def block_flags(structure, first_row, count):
    blocks = (first_row + jnp.arange(count, dtype=jnp.int32)) // BLK
    hits = jnp.any(blocks[:, None] == structure[None, :], axis=1)
    return hits.astype(jnp.float32)[:, None]


def panel_apart(normal, col_index, spread_count):
    row_block = lax.all_gather(normal, "col", axis=0, tiled=True)
    pieces = []
    for offset in range(spread_count):
        pieces.append(spread(row_block, "row", col_index * spread_count + offset))
    return (row_block, jnp.concatenate(pieces, axis=0))


def sweep(trailing, col_block, own_normal):
    summed = lax.psum_scatter(-product(trailing, col_block), "col", scatter_dimension=0, tiled=True)
    quad_part = product(own_normal.T, summed)
    return (summed, quad_part)


def body(
    trailing,
    factor_one,
    inverse_one,
    factor_two_top,
    factor_two,
    inverse_two,
    structure_one,
    structure_two,
):
    piece_rows = factor_one.shape[0]
    spread_count = lax.axis_size("row") // lax.axis_size("col")
    row_index = lax.axis_index("row")
    col_index = lax.axis_index("col")
    first_row = (row_index * lax.axis_size("col") + col_index) * piece_rows
    mask_one = block_flags(structure_one, first_row, piece_rows)
    mask_two = block_flags(structure_two, first_row, piece_rows)
    normal_one = mask_one * product(factor_one, inverse_one)
    normal_two = mask_two * product(factor_two, inverse_two)
    rows_one, cols_one = panel_apart(normal_one, col_index, spread_count)
    rows_two, cols_two = panel_apart(normal_two, col_index, spread_count)
    summed_one, quad_one = sweep(trailing, cols_one, normal_one)
    column_one = mask_one * summed_one
    diag_total = lax.psum(quad_one, ("row", "col"))
    diagonal_one = product(inverse_one.T, inverse_one) - diag_total
    normal_top = product(factor_two_top, inverse_two)
    summed_two, quad_two = sweep(trailing, cols_two, normal_two)
    local_part = -product(column_one, normal_top)
    column_two = mask_two * (local_part + summed_two)
    cross_total, second_total = lax.psum(
        (product(column_one.T, normal_two), product(normal_two.T, local_part) + quad_two),
        ("row", "col"),
    )
    cross_two = -(product(diagonal_one, normal_top) + cross_total)
    diagonal_two = (
        product(inverse_two.T, inverse_two) - product(normal_top.T, cross_two) - second_total
    )
    return (column_one, diagonal_one, column_two, cross_two, diagonal_two)


def solution(mesh):
    return jax.shard_map(
        body,
        mesh=mesh,
        in_specs=(
            P("row", "col"),
            P(("row", "col"), None),
            P(),
            P(),
            P(("row", "col"), None),
            P(),
            P(),
            P(),
        ),
        out_specs=(P(("row", "col"), None), P(), P(("row", "col"), None), P(), P()),
        check_vma=False,
    )
```

profile of v0, /device:TPU:0, one launch (start us, length us, event | category | flops | bytes accessed | tf_op | source)
XLA Modules:
  0.0 934.2 jit_solution(1768077847177011620)
XLA Ops:
  7.2 0.0 copy-start
  7.2 0.0 copy-start.14
  7.2 0.0 copy-start.4
  7.2 0.0 copy-start.12
  7.2 0.0 all-gather.5.cloned.1.call-start
  7.3 0.9 compare_reduce_fusion
  8.2 0.2 copy-done
  8.4 4.0 convolution_multiply_fusion
  12.4 0.0 all-gather.5.cloned.1.call-update
  12.5 0.0 all-gather.3.cloned.1.call-start
  12.5 0.0 copy-done.14
  12.5 0.1 compare_reduce_fusion.1
  12.7 2.8 convolution_multiply_fusion.1
  15.5 0.0 all-gather.3.cloned.1.call-update
  15.5 0.0 all-reduce.7.cloned.1.call-start
  15.6 34.2 %all-gather.5.cloned.1.call-done = f32[2048,512]{1,0:T(8,128)} async-done(((f32[512,512]{1,0:T(8,128)}), f32[2048,512]{1,0:T(8,128)}) %all-gather.5.cloned.1.call-update) | async-done | bytes 4194320 | tf_op jit(solution)/shard_map/all_gather | solution.py:25
  49.8 6.7 broadcast_select_fusion.1
  56.5 29.9 %all-gather.3.cloned.1.call-done = f32[2048,512]{1,0:T(8,128)} async-done(((f32[512,512]{1,0:T(8,128)}), f32[2048,512]{1,0:T(8,128)}) %all-gather.3.cloned.1.call-update) | async-done | bytes 4194320 | tf_op jit(solution)/shard_map/all_gather | solution.py:25
  86.4 6.7 broadcast_select_fusion.3
  93.2 0.0 all-reduce.7.cloned.1.call-update
  93.2 0.6 reduce-scatter.3.cloned.1.call-start
  93.8 509.4 %all-reduce.7.cloned.1.call-done = (f32[2048,512]{1,0:T(8,128)}, f32[2048,512]{1,0:T(8,128)}, f32[2048,512]{1,0:T(8,128)}, f32[2048,512]{1,0:T(8,128)}) async-done(((f32[2048,512]{1,0:T(8,128)}, f32[2048,512]{1,0:T(8,128)}, f32[2048,512]{1,0:T(8,128)}, f32[2048,512]{1,0:T(8,128)}), (f32[2048,512]{1,0:T(8,128)}, f32[2048,512]{1,0:T(8,128)}, f32[2048,512]{1,0:T(8,128)}, ...) | async-done | bytes 16777232 | tf_op jit(solution)/shard_map/psum | solution.py:11
  603.2 60.1 %negate_bitcast_fusion.1 = f32[2048,512]{1,0:T(8,128)} fusion(f32[2048,4096]{1,0:T(8,128)} %param.8, f32[2048,512]{1,0:T(8,128)} %get-tuple-element.8, f32[2048,512]{1,0:T(8,128)} %get-tuple-element.9), kind=kOutput, calls=%fused_computation.9 | convolution fusion | flops 51542753280 | bytes 46137344 | tf_op jit(solution)/shard_map/dot_general | solution.py:15
  663.3 0.0 reduce-scatter.3.cloned.1.call-update
  663.4 0.2 reduce-scatter.5.cloned.1.call-start
  663.6 60.1 %negate_bitcast_fusion = f32[2048,512]{1,0:T(8,128)} fusion(f32[2048,4096]{1,0:T(8,128)} %param.8, f32[2048,512]{1,0:T(8,128)} %get-tuple-element.10, f32[2048,512]{1,0:T(8,128)} %get-tuple-element.11), kind=kOutput, calls=%fused_computation.8 | convolution fusion | flops 51542753280 | bytes 46137344 | tf_op jit(solution)/shard_map/dot_general | solution.py:15
  723.7 0.0 reduce-scatter.5.cloned.1.call-update
  723.7 0.3 all-reduce.5.cloned.1.call-start
  724.0 3.1 fusion.20
  727.1 0.0 reduce-scatter.3.cloned.1.call-done
  727.1 1.5 broadcast_multiply_fusion
  728.6 0.0 copy-start.2
  728.6 1.0 copy-done.2
  729.6 2.8 fusion.21
  732.4 35.1 %reduce-scatter.5.cloned.1.call-done = f32[512,512]{1,0:T(8,128)} async-done(((f32[2048,512]{1,0:T(8,128)}), f32[512,512]{1,0:T(8,128)}) %reduce-scatter.5.cloned.1.call-update) | async-done | bytes 1048592 | tf_op jit(solution)/shard_map/reduce_scatter | solution.py:33
  767.5 4.5 add_multiply_fusion
  772.0 1.9 fusion.23
  773.9 2.9 fusion.19
  776.8 2.9 convolution_add_fusion
  779.6 0.0 all-reduce.5.cloned.1.call-update
  779.6 3.1 fusion.22
  782.7 136.1 %all-reduce.5.cloned.1.call-done = (f32[512,512]{1,0:T(8,128)}, f32[512,512]{1,0:T(8,128)}, f32[512,512]{1,0:T(8,128)}) async-done(((f32[512,512]{1,0:T(8,128)}, f32[512,512]{1,0:T(8,128)}, f32[512,512]{1,0:T(8,128)}), (f32[512,512]{1,0:T(8,128)}, f32[512,512]{1,0:T(8,128)}, f32[512,512]{1,0:T(8,128)})) %all-reduce.5.cloned.1.call-update) | async-done | bytes 3145744 | tf_op jit(solution)/shard_map/psum | solution.py:61
  918.9 0.0 copy-done.5
  918.9 3.3 convolution_subtract_fusion.1
  922.2 0.0 copy-start.10
  922.2 1.9 fusion.13
  924.1 0.0 copy-start.9
  924.2 2.9 fusion.12
  (22 shorter events, 0.1 us)
Async XLA Ops:
  7.2 1.2 copy-start
  7.2 5.3 copy-start.14
  7.2 5.5 copy-start.4
  7.2 5.5 copy-start.12
  7.2 42.6 %all-gather.5.cloned.1.call-start = ((), (), s32[]{:S(2)}) async-start(), calls=%async_computation.4 | async-start | bytes 5242880 | tf_op jit(solution)/shard_map/all_gather | solution.py:25
  12.5 74.0 %all-gather.3.cloned.1.call-start = ((), (), s32[]{:S(2)}) async-start(), calls=%async_computation.2 | async-start | bytes 5242880 | tf_op jit(solution)/shard_map/all_gather | solution.py:25
  15.5 587.7 %all-reduce.7.cloned.1.call-start = ((), (), s32[]{:S(2)}) async-start(), calls=%async_computation.7 | async-start | bytes 33554432 | tf_op jit(solution)/shard_map/psum | solution.py:11
  93.2 633.9 %reduce-scatter.3.cloned.1.call-start = ((), (), s32[]{:S(2)}) async-start(), calls=%async_computation.3 | async-start | bytes 5242880 | tf_op jit(solution)/shard_map/reduce_scatter | solution.py:33
  663.4 104.1 %reduce-scatter.5.cloned.1.call-start = ((), (), s32[]{:S(2)}) async-start(), calls=%async_computation.5 | async-start | bytes 5242880 | tf_op jit(solution)/shard_map/reduce_scatter | solution.py:33
  723.7 5.9 copy-start.1
  723.7 195.2 %all-reduce.5.cloned.1.call-start = ((), (), s32[]{:S(2)}) async-start(), calls=%async_computation.6 | async-start | bytes 6291456 | tf_op jit(solution)/shard_map/psum | solution.py:61
  728.6 1.0 copy-start.2
  767.5 6.4 copy-start.3
  767.5 6.4 copy-start.7
  772.0 4.8 copy-start.8
  779.6 139.3 %copy-start.5 = (f32[512,512]{1,0:T(8,128)S(1)}, f32[512,512]{1,0:T(8,128)}, u32[]{:S(2)}) copy-start(f32[512,512]{1,0:T(8,128)} %param.10) | copy-start | bytes 3145732
  918.9 3.3 copy-start.13
  918.9 5.2 copy-start.6
  918.9 5.3 copy-start.11
  922.2 4.9 copy-start.10
  924.1 3.0 copy-start.9
Sparse Core Ops, SparseCore 0:
  12.6 37.1 all-gather.4
  51.9 34.4 all-gather.2
  93.3 509.8 all-reduce.6
  663.5 43.6 reduce-scatter.2
  723.8 43.6 reduce-scatter.4
  779.8 139.0 all-reduce.4
where the time goes:
time: 939 us; the launch traced here: 934 us
  waiting for transfers between devices  745 us (79%)
  matrix products  156 us (17%)
  other arithmetic  16 us (2%)
  between operations  14.6 us (2%)
    psum x1, waiting for transfers between devices, spread(): return lax.psum(jnp.where(mine, x, jnp.zeros_like(x)), axis)  509 us
    dot_general x14, matrix products, product(): jnp.dot(left, right, precision=lax.Precision.HIGHEST, preferred_element_t...  156 us
    psum x1, waiting for transfers between devices, body(): diag_total = lax.psum(quad_one, ('row', 'col'))  136 us
    all_gather x2, waiting for transfers between devices, panel_apart(): row_block = lax.all_gather(normal, 'col', axis=0, tiled=True)  64.1 us
    reduce_scatter x2, waiting for transfers between devices, sweep(): lax.psum_scatter(-product(trailing, col_block), 'col', scatter_dimension=...  35.1 us
  transfers between devices with their start and end apart: 6, of which 5 were waited for; matrix products, arithmetic and copies ran while one was open for 9% of the time, Pallas kernels for 0%

commit v1 on v0

v1 whole, which is shorter than its diff:
```python
import jax
import jax.numpy as jnp
from jax import lax
from jax.sharding import PartitionSpec as P

BLK = 128


def product(left, right):
    return jnp.dot(left, right, precision=lax.Precision.HIGHEST, preferred_element_type=jnp.float32)


def big_product(left, right):
    return jnp.dot(left, right, precision=lax.Precision.HIGH, preferred_element_type=jnp.float32)


def block_flags(structure, first_row, count):
    blocks = (first_row + jnp.arange(count, dtype=jnp.int32)) // BLK
    hits = jnp.any(blocks[:, None] == structure[None, :], axis=1)
    return hits.astype(jnp.float32)[:, None]


def column_panel(normal, turn):
    rows, cols = lax.axis_size("row"), lax.axis_size("col")
    if rows == 8 and cols == 4:
        return column_panel_torus(normal, turn)
    moves = [(p, (p % rows) * cols + p // rows) for p in range(rows * cols)]
    piece = lax.ppermute(normal, ("row", "col"), moves)
    return lax.all_gather(piece, "row", axis=0, tiled=True)


def column_panel_torus(normal, turn):
    rows = lax.axis_size("row")
    depth = rows // 2
    moves = []
    for z in range(depth):
        for y in range(2):
            for x in range(2):
                for core in range(2):
                    off = 2 * core + (0 if x == z // 2 else 1)
                    target = (z + off) % depth
                    moves.append(((2 * z + y) * 4 + 2 * x + core, (2 * target + y) * 4 + z))
    across = [(r, r ^ 1) for r in range(rows)]
    up = [(r, (r + 2) % rows) for r in range(rows)]
    down = [(r, (r - 2) % rows) for r in range(rows)]
    half = normal.shape[0] // 2

    def go(x, way):
        return lax.ppermute(x, "row", way)

    a0 = lax.ppermute(normal[:half], ("row", "col"), moves)
    b0 = lax.ppermute(normal[half:], ("row", "col"), moves)
    a1 = go(a0, across)
    b_up, b_down = go(b0, up), go(b0, down)
    a0_up, a0_down = go(a0, up), go(a0, down)
    c0 = go(b0, across)
    a1_up, a1_down = go(a1, up), go(a1, down)
    c_up, c_down = go(b_up, across), go(b_down, across)
    b_far = go(b_up, up) if turn == 0 else go(b_down, down)
    a0_far = go(a0_up, up)
    a1_far = go(a1_down, down)
    c_far = go(b_far, across)

    z, y = lax.axis_index("row") // 2, lax.axis_index("row") % 2
    c = lax.axis_index("col")

    def place(step, other):
        off = (z - step - c) % depth
        x = jnp.where(off % 2 == 0, c // 2, 1 - c // 2)
        return 4 * ((y + other) % 2) + 2 * x + off // 2

    parts = (
        (a0, b0, 0, 0), (a1, c0, 0, 1),
        (a0_up, b_up, 1, 0), (a1_up, c_up, 1, 1),
        (a0_down, b_down, -1, 0), (a1_down, c_down, -1, 1),
        (a0_far, b_far, 2, 0), (a1_far, c_far, 2, 1),
    )
    panel = jnp.zeros((rows * 2 * half, normal.shape[1]), normal.dtype)
    for first, second, step, other in parts:
        at = place(step, other) * (2 * half)
        panel = lax.dynamic_update_slice(panel, first, (at, 0))
        panel = lax.dynamic_update_slice(panel, second, (at + half, 0))
    return lax.optimization_barrier(panel)


def total_over_all(x):
    return lax.psum(x, ("row", "col"))


def sweep(trailing, col_block):
    part = -big_product(trailing, col_block)
    return lax.psum_scatter(part, "col", scatter_dimension=0, tiled=True)


def body(
    trailing,
    factor_one,
    inverse_one,
    factor_two_top,
    factor_two,
    inverse_two,
    structure_one,
    structure_two,
):
    piece_rows = factor_one.shape[0]
    row_index = lax.axis_index("row")
    col_index = lax.axis_index("col")
    first_row = (row_index * lax.axis_size("col") + col_index) * piece_rows
    mask_one = block_flags(structure_one, first_row, piece_rows)
    mask_two = block_flags(structure_two, first_row, piece_rows)
    normal_one = mask_one * product(factor_one, inverse_one)
    cols_one = column_panel(normal_one, 0)
    normal_two = mask_two * product(factor_two, inverse_two)
    cols_two = column_panel(normal_two, 1)
    normal_top = product(factor_two_top, inverse_two)
    summed_one = sweep(trailing, cols_one)
    summed_two = sweep(trailing, cols_two)
    column_one = mask_one * summed_one
    both = product(column_one.T, jnp.concatenate([normal_one, normal_two], axis=1))
    column_two = mask_two * (summed_two - product(column_one, normal_top))
    second = product(normal_two.T, column_two)
    totals = total_over_all(jnp.concatenate([both, second], axis=1))
    width = normal_one.shape[1]
    diagonal_one = product(inverse_one.T, inverse_one) - totals[:, :width].T
    cross_two = -(product(diagonal_one, normal_top) + totals[:, width : 2 * width])
    diagonal_two = (
        product(inverse_two.T, inverse_two)
        - product(normal_top.T, cross_two)
        - totals[:, 2 * width :]
    )
    return (column_one, diagonal_one, column_two, cross_two, diagonal_two)


def solution(mesh):
    return jax.shard_map(
        body,
        mesh=mesh,
        in_specs=(
            P("row", "col"),
            P(("row", "col"), None),
            P(),
            P(),
            P(("row", "col"), None),
            P(),
            P(),
            P(),
        ),
        out_specs=(P(("row", "col"), None), P(), P(("row", "col"), None), P(), P()),
        check_vma=False,
    )
```

time: 939 us -> 582 us (0.62)
  waiting for transfers between devices: 745 us -> 283 us
  starting transfers between devices: 1.16 us -> 132 us
  matrix products: 156 us -> 101 us
  local copies, waits for them, and re-layouts: 1.23 us -> 34.5 us
    psum x2 -> x1, waiting for transfers between devices: 646 us -> 131 us  [total_over_all(): return lax.psum(x, ('row', 'col'))]
    ppermute x0 -> x32, starting transfers between devices: none -> 132 us  [the longest x28 125 us: go(): return lax.ppermute(x, 'row', way)]
    dot_general x14 -> x10, matrix products: 156 us -> 34.8 us  [product(): jnp.dot(left, right, precision=lax.Precision.HIGHEST, preferred_element_t...]
    ppermute x0 -> x32, waiting for transfers between devices: none -> 82.6 us  [the longest x28 82.6 us: go(): return lax.ppermute(x, 'row', way)]
    dot_general x0 -> x2, matrix products: none -> 66.3 us  [big_product(): jnp.dot(left, right, precision=lax.Precision.HIGH, preferred_element_type...]
    all_gather x2 -> x0, waiting for transfers between devices: 64.1 us -> none  [panel_apart(): row_block = lax.all_gather(normal, 'col', axis=0, tiled=True)]
    reduce_scatter x2, waiting for transfers between devices: 35.1 us -> 69 us  [sweep(): return lax.psum_scatter(part, 'col', scatter_dimension=0, tiled=True)]
    dynamic_update_slice x0 -> x31, local copies, waits for them, and re-layouts: none -> 16.3 us  [the longest x16 8.65 us: column_panel_torus(): panel = lax.dynamic_update_slice(panel, first, (at, 0))]
  transfers between devices with their start and end apart: 6 -> 35, of which waited for: 5 -> 14; matrix products, arithmetic and copies ran while one was open for 9% -> 14% of each run, Pallas kernels for 0% -> 0%
where the time goes in v1:
time: 582 us; the launch traced here: 574 us
  waiting for transfers between devices  283 us (49%)
  starting transfers between devices  132 us (23%)
  matrix products  101 us (17%)
  local copies, waits for them, and re-layouts  34.5 us (6%)
  between operations  14.6 us (3%)
  other arithmetic  8.31 us (1%)
    psum x1, waiting for transfers between devices, total_over_all(): return lax.psum(x, ('row', 'col'))  131 us
    ppermute x28, starting transfers between devices, go(): return lax.ppermute(x, 'row', way)  125 us
    ppermute x28, waiting for transfers between devices, go(): return lax.ppermute(x, 'row', way)  82.6 us
    reduce_scatter x2, waiting for transfers between devices, sweep(): return lax.psum_scatter(part, 'col', scatter_dimension=0, tiled=True)  69 us
    dot_general x2, matrix products, big_product(): jnp.dot(left, right, precision=lax.Precision.HIGH, preferred_element_type...  66.3 us
    dot_general x10, matrix products, product(): jnp.dot(left, right, precision=lax.Precision.HIGHEST, preferred_element_t...  34.8 us
  transfers between devices with their start and end apart: 35, of which 14 were waited for; matrix products, arithmetic and copies ran while one was open for 14% of the time, Pallas kernels for 0%

profile of v1, /device:TPU:0, one launch (start us, length us, event | category | flops | bytes accessed | tf_op | source)
XLA Modules:
  0.0 573.8 jit_solution(5273714210892511995)
XLA Ops:
  8.1 3.4 convolution_multiply_fusion.1
  14.0 1.7 collective-permute-start.1
  16.5 3.1 convolution_multiply_fusion
  21.6 1.7 collective-permute-start.16
  23.3 1.7 collective-permute-start.17
  25.0 3.0 collective-permute-start.2
  28.0 6.6 %collective-permute-start.4 = (f32[256,512]{0,1:T(8,128)}, f32[256,512]{0,1:T(8,128)S(1)}, u32[]{:S(2)}, u32[]{:S(2)}) collective-permute-start(f32[256,512]{0,1:T(8,128)} %collective-permute-done), channel_id=1, source_target_pairs={{0,8},{4,12},{8,16},{12,20},{16,24},{20,28},{24,0},{28,4},{1,9},{5... | collective-permute-start | bytes 1572872 | tf_op jit(solution)/shard_map/ppermute | solution.py:49
  37.2 16.9 %collective-permute-start.5 = (f32[256,512]{0,1:T(8,128)S(1)}, f32[256,512]{0,1:T(8,128)S(1)}, u32[]{:S(2)}, u32[]{:S(2)}) collective-permute-start(f32[256,512]{0,1:T(8,128)S(1)} %collective-permute-done.1), channel_id=1, source_target_pairs={{0,8},{4,12},{8,16},{12,20},{16,24},{20,28},{24,0},{28,4},{1,9},{5... | collective-permute-start | bytes 1572872 | tf_op jit(solution)/shard_map/ppermute | solution.py:49
  54.2 4.3 broadcast.62.clone
  59.4 1.6 collective-permute-start.18
  62.4 6.0 %collective-permute-start.20 = (f32[256,512]{0,1:T(8,128)S(1)}, f32[256,512]{0,1:T(8,128)S(1)}, u32[]{:S(2)}, u32[]{:S(2)}) collective-permute-start(f32[256,512]{0,1:T(8,128)S(1)} %collective-permute-done.16), channel_id=1, source_target_pairs={{0,8},{4,12},{8,16},{12,20},{16,24},{20,28},{24,0},{28,4},{1,9},{5... | collective-permute-start | bytes 1572872 | tf_op jit(solution)/shard_map/ppermute | solution.py:49
  68.5 9.3 %collective-permute-done.4 = f32[256,512]{0,1:T(8,128)S(1)} collective-permute-done((f32[256,512]{0,1:T(8,128)}, f32[256,512]{0,1:T(8,128)S(1)}, u32[]{:S(2)}, u32[]{:S(2)}) %collective-permute-start.4) | collective-permute-done | bytes 524320 | tf_op jit(solution)/shard_map/ppermute | solution.py:49
  77.9 10.8 %collective-permute-done.5 = f32[256,512]{0,1:T(8,128)S(1)} collective-permute-done((f32[256,512]{0,1:T(8,128)S(1)}, f32[256,512]{0,1:T(8,128)S(1)}, u32[]{:S(2)}, u32[]{:S(2)}) %collective-permute-start.5) | collective-permute-done | bytes 524320 | tf_op jit(solution)/shard_map/ppermute | solution.py:49
  91.3 3.8 collective-permute-start.8
  96.0 1.9 collective-permute-start.9
  98.0 2.1 collective-permute-done.21
  101.0 9.3 %collective-permute-done.6 = f32[256,512]{0,1:T(8,128)S(1)} collective-permute-done((f32[256,512]{0,1:T(8,128)S(1)}, f32[256,512]{0,1:T(8,128)S(1)}, u32[]{:S(2)}, u32[]{:S(2)}) %collective-permute-start.6) | collective-permute-done | bytes 524320 | tf_op jit(solution)/shard_map/ppermute | solution.py:49
  112.8 21.4 %collective-permute-start.24 = (f32[256,512]{0,1:T(8,128)S(1)}, f32[256,512]{0,1:T(8,128)S(1)}, u32[]{:S(2)}, u32[]{:S(2)}) collective-permute-start(f32[256,512]{0,1:T(8,128)S(1)} %collective-permute-done.16), channel_id=1, source_target_pairs={{0,24},{4,28},{8,0},{12,4},{16,8},{20,12},{24,16},{28,20},{1,25},{... | collective-permute-start | bytes 1572872 | tf_op jit(solution)/shard_map/ppermute | solution.py:49
  134.4 11.7 %collective-permute-done.9 = f32[256,512]{0,1:T(8,128)S(1)} collective-permute-done((f32[256,512]{0,1:T(8,128)S(1)}, f32[256,512]{0,1:T(8,128)S(1)}, u32[]{:S(2)}, u32[]{:S(2)}) %collective-permute-start.9) | collective-permute-done | bytes 524320 | tf_op jit(solution)/shard_map/ppermute | solution.py:49
  146.1 2.1 collective-permute-start.11
  148.3 24.3 %collective-permute-start.26 = (f32[256,512]{0,1:T(8,128)S(1)}, f32[256,512]{0,1:T(8,128)S(1)}, u32[]{:S(2)}, u32[]{:S(2)}) collective-permute-start(f32[256,512]{0,1:T(8,128)S(1)} %collective-permute-done.18), channel_id=1, source_target_pairs={{0,24},{4,28},{8,0},{12,4},{16,8},{20,12},{24,16},{28,20},{1,25},{... | collective-permute-start | bytes 1572872 | tf_op jit(solution)/shard_map/ppermute | solution.py:49
  176.7 2.5 collective-permute-start.27
  179.2 2.7 collective-permute-start.29
  182.0 8.4 %collective-permute-done.26 = f32[256,512]{0,1:T(8,128)S(1)} collective-permute-done((f32[256,512]{0,1:T(8,128)S(1)}, f32[256,512]{0,1:T(8,128)S(1)}, u32[]{:S(2)}, u32[]{:S(2)}) %collective-permute-start.26) | collective-permute-done | bytes 524320 | tf_op jit(solution)/shard_map/ppermute | solution.py:49
  191.4 5.3 collective-permute-done.12
  196.6 6.3 %collective-permute-start.14 = (f32[256,512]{0,1:T(8,128)S(1)}, f32[256,512]{0,1:T(8,128)S(1)}, u32[]{:S(2)}, u32[]{:S(2)}) collective-permute-start(f32[256,512]{0,1:T(8,128)S(1)} %collective-permute-done.10), channel_id=1, source_target_pairs={{0,24},{4,28},{8,0},{12,4},{16,8},{20,12},{24,16},{28,20},{1,25},{... | collective-permute-start | bytes 1572872 | tf_op jit(solution)/shard_map/ppermute | solution.py:49
  203.0 4.8 collective-permute-done.13
  207.9 18.8 %collective-permute-start.30 = (f32[256,512]{0,1:T(8,128)S(1)}, f32[256,512]{0,1:T(8,128)S(1)}, u32[]{:S(2)}, u32[]{:S(2)}) collective-permute-start(f32[256,512]{0,1:T(8,128)S(1)} %collective-permute-done.26), channel_id=1, source_target_pairs={{0,24},{4,28},{8,0},{12,4},{16,8},{20,12},{24,16},{28,20},{1,25},{... | collective-permute-start | bytes 1572872 | tf_op jit(solution)/shard_map/ppermute | solution.py:49
  226.8 2.7 collective-permute-start.15
  232.2 9.0 %collective-permute-done.14 = f32[256,512]{0,1:T(8,128)S(1)} collective-permute-done((f32[256,512]{0,1:T(8,128)S(1)}, f32[256,512]{0,1:T(8,128)S(1)}, u32[]{:S(2)}, u32[]{:S(2)}) %collective-permute-start.14) | collective-permute-done | bytes 524320 | tf_op jit(solution)/shard_map/ppermute | solution.py:49
  241.3 11.3 %collective-permute-done.30 = f32[256,512]{0,1:T(8,128)S(1)} collective-permute-done((f32[256,512]{0,1:T(8,128)S(1)}, f32[256,512]{0,1:T(8,128)S(1)}, u32[]{:S(2)}, u32[]{:S(2)}) %collective-permute-start.30) | collective-permute-done | bytes 524320 | tf_op jit(solution)/shard_map/ppermute | solution.py:49
  254.5 32.1 %negate_bitcast_fusion.1 = f32[2048,512]{0,1:T(8,128)} fusion(f32[4096,512]{0,1:T(8,128)S(1)} %get-tuple-element.20, f32[2048,4096]{1,0:T(8,128)} %param.8), kind=kOutput, calls=%fused_computation.1 | convolution fusion | flops 25770852352 | bytes 46137344 | tf_op jit(solution)/shard_map/dot_general | solution.py:14
  286.9 34.2 %negate_bitcast_fusion = f32[2048,512]{0,1:T(8,128)} fusion(f32[4096,512]{0,1:T(8,128)} %get-tuple-element.19, f32[2048,4096]{1,0:T(8,128)} %param.8), kind=kOutput, calls=%fused_computation | convolution fusion | flops 25770852352 | bytes 46137344 | tf_op jit(solution)/shard_map/dot_general | solution.py:14
  321.4 1.8 fusion.12
  323.3 32.7 %reduce-scatter.3.cloned.1.call-done = f32[512,512]{0,1:T(8,128)} async-done(((f32[2048,512]{0,1:T(8,128)}), f32[512,512]{0,1:T(8,128)}) %reduce-scatter.3.cloned.1.call-update) | async-done | bytes 1048592 | tf_op jit(solution)/shard_map/reduce_scatter | solution.py:92
  357.3 6.4 %fusion = f32[512,1024]{0,1:T(8,128)} fusion(f32[512,512]{0,1:T(8,128)S(1)} %broadcast_multiply_fusion, f32[512,512]{0,1:T(8,128)} %copy-done.1, f32[512,512]{0,1:T(8,128)} %copy-done.2), kind=kOutput, calls=%fused_computation.3 | convolution fusion | flops 3221749760 | bytes 5242880 | tf_op jit(solution)/shard_map/dot_general | solution.py:10
  363.8 2.8 fusion.13
  366.6 36.4 %reduce-scatter.5.cloned.1.call-done = f32[512,512]{0,1:T(8,128)} async-done(((f32[2048,512]{0,1:T(8,128)}), f32[512,512]{0,1:T(8,128)}) %reduce-scatter.5.cloned.1.call-update) | async-done | bytes 1048592 | tf_op jit(solution)/shard_map/reduce_scatter | solution.py:92
  403.0 1.8 subtract_multiply_fusion
  405.7 3.1 fusion.14
  408.8 3.6 pad_maximum_fusion
  412.4 2.9 fusion.15
  415.3 2.8 copy.28
  419.4 131.3 %all-reduce.2.cloned.1.call-done = f32[512,1536]{0,1:T(8,128)} async-done(((f32[512,1536]{0,1:T(8,128)}), f32[512,1536]{0,1:T(8,128)}) %all-reduce.2.cloned.1.call-update) | async-done | bytes 3145744 | tf_op jit(solution)/shard_map/psum | solution.py:87
  550.7 3.7 convolution_subtract_fusion.1
  555.4 3.1 fusion.5
  559.8 4.4 fusion.4
  564.2 2.5 copy.30
  (96 shorter events, 34.7 us)
Async XLA Ops:
  7.2 9.3 %copy-start = (f32[512,512]{1,0:T(8,128)S(1)}, f32[512,512]{1,0:T(8,128)}, u32[]{:S(2)}) copy-start(f32[512,512]{1,0:T(8,128)} %param.13) | copy-start | bytes 3145732
  7.2 348.8 %reduce-scatter.3.cloned.1.call-start = ((), (), s32[]{:S(2)}) async-start(), calls=%async_computation.2 | async-start | bytes 5242880 | tf_op jit(solution)/shard_map/reduce_scatter | solution.py:92
  11.5 4.9 copy-start.2
  12.5 12.5 %collective-permute-start = (f32[256,512]{0,1:T(8,128)S(1)}, f32[256,512]{0,1:T(8,128)}, u32[]{:S(2)}, u32[]{:S(2)}) collective-permute-start(f32[256,512]{0,1:T(8,128)S(1)} %get-tuple-element.18), channel_id=1, source_target_pairs={{0,0},{1,16},{2,8},{3,24},{4,4},{5,20},{6,12},{7,28},{8,9},{9,25},... | collective-permute-start | bytes 1572872 | tf_op jit(solution)/shard_map/ppermute | solution.py:51
  14.0 20.6 %collective-permute-start.1 = (f32[256,512]{0,1:T(8,128)}, f32[256,512]{0,1:T(8,128)S(1)}, u32[]{:S(2)}, u32[]{:S(2)}) collective-permute-start(f32[256,512]{0,1:T(8,128)} %get-tuple-element.17), channel_id=1, source_target_pairs={{0,0},{1,16},{2,8},{3,24},{4,4},{5,20},{6,12},{7,28},{8,9},{9,25},... | collective-permute-start | bytes 1572872 | tf_op jit(solution)/shard_map/ppermute | solution.py:52
  19.6 1.0 copy-start.1
  21.6 15.6 %collective-permute-start.16 = (f32[256,512]{0,1:T(8,128)}, f32[256,512]{0,1:T(8,128)S(1)}, u32[]{:S(2)}, u32[]{:S(2)}) collective-permute-start(f32[256,512]{0,1:T(8,128)} %get-tuple-element.16), channel_id=1, source_target_pairs={{0,0},{1,16},{2,8},{3,24},{4,4},{5,20},{6,12},{7,28},{8,9},{9,25},... | collective-permute-start | bytes 1572872 | tf_op jit(solution)/shard_map/ppermute | solution.py:51
  23.3 36.1 %collective-permute-start.17 = (f32[256,512]{0,1:T(8,128)}, f32[256,512]{0,1:T(8,128)S(1)}, u32[]{:S(2)}, u32[]{:S(2)}) collective-permute-start(f32[256,512]{0,1:T(8,128)} %get-tuple-element.15), channel_id=1, source_target_pairs={{0,0},{1,16},{2,8},{3,24},{4,4},{5,20},{6,12},{7,28},{8,9},{9,25},... | collective-permute-start | bytes 1572872 | tf_op jit(solution)/shard_map/ppermute | solution.py:52
  25.0 36.8 %collective-permute-start.2 = (f32[256,512]{0,1:T(8,128)}, f32[256,512]{0,1:T(8,128)S(1)}, u32[]{:S(2)}, u32[]{:S(2)}) collective-permute-start(f32[256,512]{0,1:T(8,128)} %collective-permute-done), channel_id=1, source_target_pairs={{0,4},{4,0},{8,12},{12,8},{16,20},{20,16},{24,28},{28,24},{1,5},{5... | collective-permute-start | bytes 1572872 | tf_op jit(solution)/shard_map/ppermute | solution.py:49
  28.0 49.8 %collective-permute-start.4 = (f32[256,512]{0,1:T(8,128)}, f32[256,512]{0,1:T(8,128)S(1)}, u32[]{:S(2)}, u32[]{:S(2)}) collective-permute-start(f32[256,512]{0,1:T(8,128)} %collective-permute-done), channel_id=1, source_target_pairs={{0,8},{4,12},{8,16},{12,20},{16,24},{20,28},{24,0},{28,4},{1,9},{5... | collective-permute-start | bytes 1572872 | tf_op jit(solution)/shard_map/ppermute | solution.py:49
  34.6 27.8 %collective-permute-start.3 = (f32[256,512]{0,1:T(8,128)S(1)}, f32[256,512]{0,1:T(8,128)S(1)}, u32[]{:S(2)}, u32[]{:S(2)}) collective-permute-start(f32[256,512]{0,1:T(8,128)S(1)} %collective-permute-done.1), channel_id=1, source_target_pairs={{0,4},{4,0},{8,12},{12,8},{16,20},{20,16},{24,28},{28,24},{1,5},{5... | collective-permute-start | bytes 1572872 | tf_op jit(solution)/shard_map/ppermute | solution.py:49
  37.2 51.4 %collective-permute-start.5 = (f32[256,512]{0,1:T(8,128)S(1)}, f32[256,512]{0,1:T(8,128)S(1)}, u32[]{:S(2)}, u32[]{:S(2)}) collective-permute-start(f32[256,512]{0,1:T(8,128)S(1)} %collective-permute-done.1), channel_id=1, source_target_pairs={{0,8},{4,12},{8,16},{12,20},{16,24},{20,28},{24,0},{28,4},{1,9},{5... | collective-permute-start | bytes 1572872 | tf_op jit(solution)/shard_map/ppermute | solution.py:49
  59.4 29.4 %collective-permute-start.18 = (f32[256,512]{0,1:T(8,128)S(1)}, f32[256,512]{0,1:T(8,128)S(1)}, u32[]{:S(2)}, u32[]{:S(2)}) collective-permute-start(f32[256,512]{0,1:T(8,128)S(1)} %collective-permute-done.16), channel_id=1, source_target_pairs={{0,4},{4,0},{8,12},{12,8},{16,20},{20,16},{24,28},{28,24},{1,5},{5... | collective-permute-start | bytes 1572872 | tf_op jit(solution)/shard_map/ppermute | solution.py:49
  61.8 29.5 %collective-permute-start.19 = (f32[256,512]{0,1:T(8,128)S(1)}, f32[256,512]{0,1:T(8,128)S(1)}, u32[]{:S(2)}, u32[]{:S(2)}) collective-permute-start(f32[256,512]{0,1:T(8,128)S(1)} %collective-permute-done.17), channel_id=1, source_target_pairs={{0,4},{4,0},{8,12},{12,8},{16,20},{20,16},{24,28},{28,24},{1,5},{5... | collective-permute-start | bytes 1572872 | tf_op jit(solution)/shard_map/ppermute | solution.py:49
  62.4 33.6 %collective-permute-start.20 = (f32[256,512]{0,1:T(8,128)S(1)}, f32[256,512]{0,1:T(8,128)S(1)}, u32[]{:S(2)}, u32[]{:S(2)}) collective-permute-start(f32[256,512]{0,1:T(8,128)S(1)} %collective-permute-done.16), channel_id=1, source_target_pairs={{0,8},{4,12},{8,16},{12,20},{16,24},{20,28},{24,0},{28,4},{1,9},{5... | collective-permute-start | bytes 1572872 | tf_op jit(solution)/shard_map/ppermute | solution.py:49
  77.8 22.3 %collective-permute-start.21 = (f32[256,512]{0,1:T(8,128)S(1)}, f32[256,512]{0,1:T(8,128)S(1)}, u32[]{:S(2)}, u32[]{:S(2)}) collective-permute-start(f32[256,512]{0,1:T(8,128)S(1)} %collective-permute-done.17), channel_id=1, source_target_pairs={{0,8},{4,12},{8,16},{12,20},{16,24},{20,28},{24,0},{28,4},{1,9},{5... | collective-permute-start | bytes 1572872 | tf_op jit(solution)/shard_map/ppermute | solution.py:49
  88.7 21.6 %collective-permute-start.6 = (f32[256,512]{0,1:T(8,128)S(1)}, f32[256,512]{0,1:T(8,128)S(1)}, u32[]{:S(2)}, u32[]{:S(2)}) collective-permute-start(f32[256,512]{0,1:T(8,128)S(1)} %collective-permute-done.2), channel_id=1, source_target_pairs={{0,8},{4,12},{8,16},{12,20},{16,24},{20,28},{24,0},{28,4},{1,9},{5... | collective-permute-start | bytes 1572872 | tf_op jit(solution)/shard_map/ppermute | solution.py:49
  88.8 23.9 %collective-permute-start.7 = (f32[256,512]{0,1:T(8,128)S(1)}, f32[256,512]{0,1:T(8,128)S(1)}, u32[]{:S(2)}, u32[]{:S(2)}) collective-permute-start(f32[256,512]{0,1:T(8,128)S(1)} %collective-permute-done.5), channel_id=1, source_target_pairs={{0,4},{4,0},{8,12},{12,8},{16,20},{20,16},{24,28},{28,24},{1,5},{5... | collective-permute-start | bytes 1572872 | tf_op jit(solution)/shard_map/ppermute | solution.py:49
  91.3 42.9 %collective-permute-start.8 = (f32[256,512]{0,1:T(8,128)}, f32[256,512]{0,1:T(8,128)S(1)}, u32[]{:S(2)}, u32[]{:S(2)}) collective-permute-start(f32[256,512]{0,1:T(8,128)} %collective-permute-done), channel_id=1, source_target_pairs={{0,24},{4,28},{8,0},{12,4},{16,8},{20,12},{24,16},{28,20},{1,25},{... | collective-permute-start | bytes 1572872 | tf_op jit(solution)/shard_map/ppermute | solution.py:49
  96.0 50.0 %collective-permute-start.9 = (f32[256,512]{0,1:T(8,128)S(1)}, f32[256,512]{0,1:T(8,128)S(1)}, u32[]{:S(2)}, u32[]{:S(2)}) collective-permute-start(f32[256,512]{0,1:T(8,128)S(1)} %collective-permute-done.1), channel_id=1, source_target_pairs={{0,24},{4,28},{8,0},{12,4},{16,8},{20,12},{24,16},{28,20},{1,25},{... | collective-permute-start | bytes 1572872 | tf_op jit(solution)/shard_map/ppermute | solution.py:49
  100.1 46.0 %collective-permute-start.22 = (f32[256,512]{0,1:T(8,128)S(1)}, f32[256,512]{0,1:T(8,128)S(1)}, u32[]{:S(2)}, u32[]{:S(2)}) collective-permute-start(f32[256,512]{0,1:T(8,128)S(1)} %collective-permute-done.18), channel_id=1, source_target_pairs={{0,8},{4,12},{8,16},{12,20},{16,24},{20,28},{24,0},{28,4},{1,9},{5... | collective-permute-start | bytes 1572872 | tf_op jit(solution)/shard_map/ppermute | solution.py:49
  110.3 38.0 %collective-permute-start.23 = (f32[256,512]{0,1:T(8,128)S(1)}, f32[256,512]{0,1:T(8,128)S(1)}, u32[]{:S(2)}, u32[]{:S(2)}) collective-permute-start(f32[256,512]{0,1:T(8,128)S(1)} %collective-permute-done.21), channel_id=1, source_target_pairs={{0,4},{4,0},{8,12},{12,8},{16,20},{20,16},{24,28},{28,24},{1,5},{5... | collective-permute-start | bytes 1572872 | tf_op jit(solution)/shard_map/ppermute | solution.py:49
  112.8 61.6 %collective-permute-start.24 = (f32[256,512]{0,1:T(8,128)S(1)}, f32[256,512]{0,1:T(8,128)S(1)}, u32[]{:S(2)}, u32[]{:S(2)}) collective-permute-start(f32[256,512]{0,1:T(8,128)S(1)} %collective-permute-done.16), channel_id=1, source_target_pairs={{0,24},{4,28},{8,0},{12,4},{16,8},{20,12},{24,16},{28,20},{1,25},{... | collective-permute-start | bytes 1572872 | tf_op jit(solution)/shard_map/ppermute | solution.py:49
  134.3 41.0 %collective-permute-start.25 = (f32[256,512]{0,1:T(8,128)S(1)}, f32[256,512]{0,1:T(8,128)S(1)}, u32[]{:S(2)}, u32[]{:S(2)}) collective-permute-start(f32[256,512]{0,1:T(8,128)S(1)} %collective-permute-done.17), channel_id=1, source_target_pairs={{0,24},{4,28},{8,0},{12,4},{16,8},{20,12},{24,16},{28,20},{1,25},{... | collective-permute-start | bytes 1572872 | tf_op jit(solution)/shard_map/ppermute | solution.py:49
  146.1 30.6 %collective-permute-start.10 = (f32[256,512]{0,1:T(8,128)S(1)}, f32[256,512]{0,1:T(8,128)S(1)}, u32[]{:S(2)}, u32[]{:S(2)}) collective-permute-start(f32[256,512]{0,1:T(8,128)S(1)} %collective-permute-done.2), channel_id=1, source_target_pairs={{0,24},{4,28},{8,0},{12,4},{16,8},{20,12},{24,16},{28,20},{1,25},{... | collective-permute-start | bytes 1572872 | tf_op jit(solution)/shard_map/ppermute | solution.py:49
  146.1 33.1 %collective-permute-start.11 = (f32[256,512]{0,1:T(8,128)S(1)}, f32[256,512]{0,1:T(8,128)S(1)}, u32[]{:S(2)}, u32[]{:S(2)}) collective-permute-start(f32[256,512]{0,1:T(8,128)S(1)} %collective-permute-done.9), channel_id=1, source_target_pairs={{0,4},{4,0},{8,12},{12,8},{16,20},{20,16},{24,28},{28,24},{1,5},{5... | collective-permute-start | bytes 1572872 | tf_op jit(solution)/shard_map/ppermute | solution.py:49
  148.3 42.1 %collective-permute-start.26 = (f32[256,512]{0,1:T(8,128)S(1)}, f32[256,512]{0,1:T(8,128)S(1)}, u32[]{:S(2)}, u32[]{:S(2)}) collective-permute-start(f32[256,512]{0,1:T(8,128)S(1)} %collective-permute-done.18), channel_id=1, source_target_pairs={{0,24},{4,28},{8,0},{12,4},{16,8},{20,12},{24,16},{28,20},{1,25},{... | collective-permute-start | bytes 1572872 | tf_op jit(solution)/shard_map/ppermute | solution.py:49
  174.4 22.3 %collective-permute-start.12 = (f32[256,512]{0,1:T(8,128)S(1)}, f32[256,512]{0,1:T(8,128)S(1)}, u32[]{:S(2)}, u32[]{:S(2)}) collective-permute-start(f32[256,512]{0,1:T(8,128)S(1)} %collective-permute-done.4), channel_id=1, source_target_pairs={{0,8},{4,12},{8,16},{12,20},{16,24},{20,28},{24,0},{28,4},{1,9},{5... | collective-permute-start | bytes 1572872 | tf_op jit(solution)/shard_map/ppermute | solution.py:49
  175.3 32.6 %collective-permute-start.13 = (f32[256,512]{0,1:T(8,128)S(1)}, f32[256,512]{0,1:T(8,128)S(1)}, u32[]{:S(2)}, u32[]{:S(2)}) collective-permute-start(f32[256,512]{0,1:T(8,128)S(1)} %collective-permute-done.5), channel_id=1, source_target_pairs={{0,8},{4,12},{8,16},{12,20},{16,24},{20,28},{24,0},{28,4},{1,9},{5... | collective-permute-start | bytes 1572872 | tf_op jit(solution)/shard_map/ppermute | solution.py:49
  176.7 50.1 %collective-permute-start.27 = (f32[256,512]{0,1:T(8,128)S(1)}, f32[256,512]{0,1:T(8,128)S(1)}, u32[]{:S(2)}, u32[]{:S(2)}) collective-permute-start(f32[256,512]{0,1:T(8,128)S(1)} %collective-permute-done.25), channel_id=1, source_target_pairs={{0,4},{4,0},{8,12},{12,8},{16,20},{20,16},{24,28},{28,24},{1,5},{5... | collective-permute-start | bytes 1572872 | tf_op jit(solution)/shard_map/ppermute | solution.py:49
  179.2 50.3 %collective-permute-start.29 = (f32[256,512]{0,1:T(8,128)S(1)}, f32[256,512]{0,1:T(8,128)S(1)}, u32[]{:S(2)}, u32[]{:S(2)}) collective-permute-start(f32[256,512]{0,1:T(8,128)S(1)} %collective-permute-done.25), channel_id=1, source_target_pairs={{0,24},{4,28},{8,0},{12,4},{16,8},{20,12},{24,16},{28,20},{1,25},{... | collective-permute-start | bytes 1572872 | tf_op jit(solution)/shard_map/ppermute | solution.py:49
  190.4 40.1 %collective-permute-start.28 = (f32[256,512]{0,1:T(8,128)S(1)}, f32[256,512]{0,1:T(8,128)S(1)}, u32[]{:S(2)}, u32[]{:S(2)}) collective-permute-start(f32[256,512]{0,1:T(8,128)S(1)} %collective-permute-done.20), channel_id=1, source_target_pairs={{0,8},{4,12},{8,16},{12,20},{16,24},{20,28},{24,0},{28,4},{1,9},{5... | collective-permute-start | bytes 1572872 | tf_op jit(solution)/shard_map/ppermute | solution.py:49
  196.6 44.6 %collective-permute-start.14 = (f32[256,512]{0,1:T(8,128)S(1)}, f32[256,512]{0,1:T(8,128)S(1)}, u32[]{:S(2)}, u32[]{:S(2)}) collective-permute-start(f32[256,512]{0,1:T(8,128)S(1)} %collective-permute-done.10), channel_id=1, source_target_pairs={{0,24},{4,28},{8,0},{12,4},{16,8},{20,12},{24,16},{28,20},{1,25},{... | collective-permute-start | bytes 1572872 | tf_op jit(solution)/shard_map/ppermute | solution.py:49
  207.9 44.7 %collective-permute-start.30 = (f32[256,512]{0,1:T(8,128)S(1)}, f32[256,512]{0,1:T(8,128)S(1)}, u32[]{:S(2)}, u32[]{:S(2)}) collective-permute-start(f32[256,512]{0,1:T(8,128)S(1)} %collective-permute-done.26), channel_id=1, source_target_pairs={{0,24},{4,28},{8,0},{12,4},{16,8},{20,12},{24,16},{28,20},{1,25},{... | collective-permute-start | bytes 1572872 | tf_op jit(solution)/shard_map/ppermute | solution.py:49
  226.8 26.7 %collective-permute-start.15 = (f32[256,512]{0,1:T(8,128)S(1)}, f32[256,512]{0,1:T(8,128)S(1)}, u32[]{:S(2)}, u32[]{:S(2)}) collective-permute-start(f32[256,512]{0,1:T(8,128)S(1)} %collective-permute-done.13), channel_id=1, source_target_pairs={{0,4},{4,0},{8,12},{12,8},{16,20},{20,16},{24,28},{28,24},{1,5},{5... | collective-permute-start | bytes 1572872 | tf_op jit(solution)/shard_map/ppermute | solution.py:49
  229.5 24.0 %collective-permute-start.31 = (f32[256,512]{0,1:T(8,128)S(1)}, f32[256,512]{0,1:T(8,128)S(1)}, u32[]{:S(2)}, u32[]{:S(2)}) collective-permute-start(f32[256,512]{0,1:T(8,128)S(1)} %collective-permute-done.29), channel_id=1, source_target_pairs={{0,4},{4,0},{8,12},{12,8},{16,20},{20,16},{24,28},{28,24},{1,5},{5... | collective-permute-start | bytes 1572872 | tf_op jit(solution)/shard_map/ppermute | solution.py:49
  286.6 116.4 %reduce-scatter.5.cloned.1.call-start = ((), (), s32[]{:S(2)}) async-start(), calls=%async_computation.3 | async-start | bytes 5242880 | tf_op jit(solution)/shard_map/reduce_scatter | solution.py:92
  286.9 34.6 %copy-start.5 = (f32[512,512]{1,0:T(8,128)S(1)}, f32[512,512]{1,0:T(8,128)}, u32[]{:S(2)}) copy-start(f32[512,512]{1,0:T(8,128)} %param.11) | copy-start | bytes 3145732
  321.1 229.6 %all-reduce.2.cloned.1.call-start = ((), (), s32[]{:S(2)}) async-start(), calls=%async_computation.4 | async-start | bytes 6291456 | tf_op jit(solution)/shard_map/psum | solution.py:87
  404.7 1.0 copy-start.3
  554.4 1.0 copy-start.4
Sparse Core Ops, SparseCore 0:
  286.7 69.1 reduce-scatter.2
  358.5 44.4 reduce-scatter.4
  412.5 138.1 all-reduce.1
